TPU v7x, 512 devices: a whole 4x4x16 slice. The times are simulated.
512 devices in a mesh: head: 8 (over x, core), seq: 64 (over z, y).
Axes of the slice: x: 4, y: 4, z: 16, core: 2. Of those that a mesh axis runs over, the one named last changes fastest.
Arguments:
- activations: bfloat16 [8192, 4096], P('seq'), may hold values from -6 to 6
- w_query: bfloat16 [3, 4096, 2048], P(None, 'seq', 'head'), may hold values from -32 to 32
- w_keyval: bfloat16 [3, 4096, 1024], P(None, 'seq'), may hold values from -32 to 32
- q_gain: float32 [3, 2048], P(None, 'head'), may hold values from 0.1 to 1.9
- k_gain: float32 [3, 512], replicated, may hold values from 0.1 to 1.9
- stream_ids: int32 [8192], P('seq'), may hold values from 0 to 2
- local_times: int32 [8192], P('seq'), may hold values from 0 to 31
- block_map: int32 [128], replicated, may hold values from 0 to 127, each once
Outputs:
- attended: bfloat16 [8192, 2048], P('seq', 'head')
Inputs may be any that keep to these rules, and one draw needn't show every extreme that they name: `block_map`: a permutation of the block indices.
All inputs are finite; a program needn't handle non-finite values.
Results may differ from a plain program's by a relative error of at most 0.012.
The roundings to bfloat16 on the way count: a program that leaves them out, or rounds other values in their place, can miss the bound.
Values may be sent and summed in bfloat16 or wider, within the bound.
A program may use at most 64 MiB of HBM per device.

v0:
```python
import math

import jax
import jax.numpy as jnp
from jax import lax
from jax.sharding import PartitionSpec as P

HEADS = 16
KV_HEADS = 4
HEAD_DIM = 128
STREAMS = 3
FRAMES = 32


epsilon = 1e-06


def sent_together(arrays, axis, dim, along):
    ends, at = ([], 0)
    for a in arrays[:-1]:
        at += a.shape[along]
        ends.append(at)
    both = jnp.concatenate(arrays, axis=along)
    return tuple(jnp.split(lax.all_gather(both, axis, axis=dim, tiled=True), ends, axis=along))


def copy_for_each(array, axis):
    length = lax.axis_size(axis)
    return lax.all_to_all(
        jnp.broadcast_to(array[None], (length, *array.shape)), axis, 0, 0, tiled=True
    )


def taken_together(array, axis):
    return copy_for_each(array, axis).sum(axis=0)


def in_one(arrays, axis):
    ends = [0]
    for a in arrays:
        ends.append(ends[-1] + a.size)
    total = taken_together(jnp.concatenate([a.ravel() for a in arrays]), axis)
    return tuple((total[b:e].reshape(a.shape) for a, b, e in zip(arrays, ends, ends[1:])))


def body(activations, w_query, w_keyval, q_gain, k_gain, stream_ids, local_times, block_map):
    row_count = activations.shape[0]
    block_rows = row_count // 2
    group_size = HEADS // KV_HEADS
    q_local = w_query.shape[2] // HEAD_DIM
    per_group = min(group_size, q_local)
    kv_local = q_local // per_group
    replicas = max(1, lax.axis_size("head") // KV_HEADS)
    head_index = lax.axis_index("head")
    first_group = head_index * q_local // group_size
    kv_weights = lax.dynamic_slice_in_dim(
        w_keyval, first_group * (2 * HEAD_DIM), kv_local * 2 * HEAD_DIM, 2
    )
    kv_gain = lax.dynamic_slice_in_dim(k_gain, first_group * HEAD_DIM, kv_local * HEAD_DIM, 1)
    position = lax.axis_index("seq")
    slot_ids = position * 2 + jnp.arange(row_count, dtype=jnp.int32) // block_rows
    slot_match = slot_ids[:, None] == jnp.arange(block_map.shape[0], dtype=jnp.int32)[None, :]
    query_times = (
        jnp.sum(jnp.where(slot_match, block_map[None, :], 0), axis=1) * FRAMES + local_times
    )
    stream_match = stream_ids[:, None] == jnp.arange(STREAMS, dtype=jnp.int32)[None, :]
    spread = activations[:, None, :] * stream_match.astype(jnp.bfloat16)[:, :, None]
    segments = sent_together((w_query, kv_weights), "seq", 1, 0)
    query_sum = jnp.einsum("rsd,sdc->rc", spread, segments[0], preferred_element_type=jnp.float32)
    pair_sum = jnp.einsum("rsd,sdc->rc", spread, segments[1], preferred_element_type=jnp.float32)
    key_value = pair_sum
    key_value = key_value.reshape(row_count, kv_local, 2, HEAD_DIM)
    keys_raw = key_value[:, :, 0].reshape(row_count, kv_local * HEAD_DIM)
    values = key_value[:, :, 1].astype(jnp.bfloat16)
    key_part = jnp.where(
        head_index % replicas == 0, jnp.sum(keys_raw * keys_raw, axis=1), jnp.float32(0.0)
    )
    query_sq, key_sq = in_one((jnp.sum(query_sum * query_sum, axis=1), key_part), "head")
    onehot = stream_match.astype(jnp.float32)
    q_scale = jnp.dot(onehot, q_gain, precision=lax.Precision.HIGHEST)
    k_scale = jnp.dot(onehot, kv_gain, precision=lax.Precision.HIGHEST)
    q_normed = (
        query_sum * lax.rsqrt(query_sq / (HEADS * HEAD_DIM) + epsilon)[:, None] * q_scale
    ).astype(jnp.bfloat16)
    q_normed = q_normed.reshape(row_count, kv_local, per_group, HEAD_DIM)
    k_normed = (
        keys_raw * lax.rsqrt(key_sq / (KV_HEADS * HEAD_DIM) + epsilon)[:, None] * k_scale
    ).astype(jnp.bfloat16)
    k_normed = k_normed.reshape(row_count, kv_local, HEAD_DIM)
    score_scale = 1.0 / math.sqrt(HEAD_DIM)
    run_max = jnp.full((row_count, kv_local, per_group), -1e30, jnp.float32)
    key_part_now, value_part, key_times = (
        *sent_together((k_normed, values), "seq", 0, 1),
        lax.all_gather(query_times, "seq", axis=0, tiled=True),
    )
    scores = (
        jnp.einsum("rkgd,nkd->rkgn", q_normed, key_part_now, preferred_element_type=jnp.float32)
        * score_scale
    )
    visible = key_times[None, None, None, :] <= query_times[:, None, None, None]
    new_max = jnp.maximum(run_max, jnp.max(jnp.where(visible, scores, -1e30), axis=3))
    exp_terms = jnp.where(visible, jnp.exp(scores - new_max[..., None]), jnp.float32(0.0))
    run_sum = jnp.sum(exp_terms, axis=3)
    weighted = jnp.einsum(
        "rkgn,nkd->rkgd",
        exp_terms.astype(jnp.bfloat16),
        value_part,
        preferred_element_type=jnp.float32,
    )
    run_max, run_sum, weighted = (new_max, run_sum, weighted)
    return (
        (weighted / run_sum[..., None])
        .reshape(row_count, kv_local * per_group * HEAD_DIM)
        .astype(jnp.bfloat16)
    )


def solution(mesh):
    placed = (
        P("seq", None),
        P(None, "seq", "head"),
        P(None, "seq", None),
        P(None, "head"),
        P(),
        P("seq"),
        P("seq"),
        P(),
    )
    return jax.shard_map(
        body, mesh=mesh, in_specs=placed, out_specs=P("seq", "head"), check_vma=False
    )
```

profile of v0, /device:TPU:4, one launch (start us, length us, event | category | flops | bytes accessed | tf_op | source)
XLA Modules:
  0.0 359.9 jit_solution(12236704924092961860)
XLA Ops:
  6.5 0.0 copy-start
  6.5 0.0 all-gather.4.cloned.1.call-start
  6.5 1.0 copy-done
  7.5 1.6 pad_maximum_fusion
  9.1 0.0 all-gather.4.cloned.1.call-update
  9.2 0.7 fusion.46
  9.8 175.3 %all-gather.4.cloned.1.call-done = bf16[6,4096,256]{2,1,0:T(8,128)(2,1)} async-done(((bf16[6,64,256]{2,1,0:T(8,128)(2,1)}), bf16[6,4096,256]{2,1,0:T(8,128)(2,1)}) %all-gather.4.cloned.1.call-update) | async-done | bytes 12582928 | tf_op jit(solution)/shard_map/all_gather | solution.py:24
  185.2 4.1 %fusion.22 = f32[128,256]{1,0:T(8,128)S(1)} fusion(bf16[6,4096,256]{2,1,0:T(8,128)(2,1)} %all-gather.4.cloned.1.call-done, bf16[128,3]{0,1:T(4,128)(2,1)S(1)} %fusion.46, bf16[128,4096]{1,0:T(8,128)(2,1)} %param.8), kind=kOutput, calls=%fused_computation.25 | convolution fusion | flops 806879232 | bytes 7471872 | tf_op jit(solution)/shard_map/rsd,sdc->rc/dot_general | solution.py:70
  189.3 0.1 reshape.129
  189.4 0.1 multiply_reduce_fusion.1
  189.6 0.0 copy-start.2
  189.6 0.0 copy-start.5
  189.6 0.0 copy-start.6
  189.6 0.0 copy-start.1
  189.6 4.0 %multiply_reduce_fusion = (f32[128]{0:T(128)S(1)}, f32[128,256]{1,0:T(8,128)S(1)}) fusion(bf16[6,4096,256]{2,1,0:T(8,128)(2,1)} %all-gather.4.cloned.1.call-done, bf16[128,3]{0,1:T(4,128)(2,1)S(1)} %fusion.46, bf16[128,4096]{1,0:T(8,128)(2,1)S(1)} %copy-done.4), kind=kOutput, calls=%fused_computation.36 | convolution fusion | flops 806944640 | bytes 7472384 | tf_op jit(solution)/shard_map/rsd,sdc->rc/dot_general | solution.py:69
  193.6 0.6 broadcast_in_dim.43
  194.2 4.8 %all-to-all-start = ((f32[8,1,256]{2,1,0:T(1,128)}), f32[8,1,256]{2,1,0:T(1,128)S(1)}, u32[]{:S(2)}, u32[]{:S(2)}) async-start(f32[8,1,256]{2,1,0:T(1,128)} %broadcast_in_dim.43), calls=%async_computation | async-start | bytes 16384 | tf_op jit(solution)/shard_map/all_to_all | solution.py:29
  199.0 0.1 slice.18
  199.1 2.8 all-to-all-done
  202.0 0.9 fusion.35
  203.0 0.6 pad_maximum_fusion.1
  203.6 0.0 all-gather.6.cloned.1.call-update
  203.6 0.2 select_reduce_fusion.1
  203.8 72.5 %all-gather = s32[64,1,128]{2,1,0:T(1,128)S(1)} all-gather(s32[1,1,128]{2,1,0:T(1,128)S(1)} %bitcast.67), channel_id=1, replica_groups=mesh['head'=8,'seq'=64] {'seq'}, dimensions={0}, use_global_device_ids=true | all-gather | bytes 33280 | tf_op jit(solution)/shard_map/all_gather | solution.py:94
  276.4 3.7 %broadcast_compare_fusion = pred[128,8192]{0,1:T(8,128)(4,1)S(1)} fusion(s32[128]{0:T(128)S(1)} %multiply_add_fusion, s32[8192]{0:T(1024)S(1)} %bitcast.64), kind=kLoop, calls=%fused_computation.19 | loop fusion | flops 1048576 | bytes 1081856 | tf_op jit(solution)/shard_map/le | solution.py:100
  280.1 0.3 fusion.33
  280.3 64.7 %all-gather.6.cloned.1.call-done = bf16[8192,2,128]{2,0,1:T(8,128)(2,1)} async-done(((bf16[128,2,128]{2,0,1:T(8,128)(2,1)}), bf16[8192,2,128]{2,0,1:T(8,128)(2,1)}) %all-gather.6.cloned.1.call-update) | async-done | bytes 4194320 | tf_op jit(solution)/shard_map/all_gather | solution.py:24
  345.0 3.4 select_reduce_fusion
  348.4 1.7 fusion.1
  350.1 0.5 copy-done.3
  350.6 1.8 fusion.39
  352.3 0.7 copy.33
  (18 shorter events, 0.2 us)
Async XLA Ops:
  6.5 1.0 copy-start
  6.5 178.6 %all-gather.4.cloned.1.call-start = ((), (), s32[]{:S(2)}) async-start(), calls=%async_computation.1 | async-start | bytes 12779520 | tf_op jit(solution)/shard_map/all_gather | solution.py:24
  9.8 179.7 %copy-start.4 = (bf16[128,4096]{1,0:T(8,128)(2,1)S(1)}, bf16[128,4096]{1,0:T(8,128)(2,1)}, u32[]{:S(2)}) copy-start(bf16[128,4096]{1,0:T(8,128)(2,1)} %param.8) | copy-start | bytes 3145732
  189.6 12.4 %copy-start.2 = (s32[128]{0:T(128)S(1)}, s32[128]{0:T(128)}, u32[]{:S(2)}) copy-start(s32[128]{0:T(128)} %param.13) | copy-start | bytes 1540
  189.6 14.0 %copy-start.5 = (s32[128]{0:T(128)S(1)}, s32[128]{0:T(128)}, u32[]{:S(2)}) copy-start(s32[128]{0:T(128)} %param.15) | copy-start | bytes 1540
  189.6 14.2 %copy-start.6 = (s32[128]{0:T(128)S(1)}, s32[128]{0:T(128)}, u32[]{:S(2)}) copy-start(s32[128]{0:T(128)} %param.14) | copy-start | bytes 1540
  189.6 90.4 %copy-start.1 = (f32[3,256]{1,0:T(4,128)S(1)}, f32[3,256]{1,0:T(4,128)}, u32[]{:S(2)}) copy-start(f32[3,256]{1,0:T(4,128)} %param.11) | copy-start | bytes 9220
  194.2 7.7 %all-to-all-start = ((f32[8,1,256]{2,1,0:T(1,128)}), f32[8,1,256]{2,1,0:T(1,128)S(1)}, u32[]{:S(2)}, u32[]{:S(2)}) async-start(f32[8,1,256]{2,1,0:T(1,128)} %broadcast_in_dim.43), calls=%async_computation | async-start | bytes 16384 | tf_op jit(solution)/shard_map/all_to_all | solution.py:29
  199.0 146.0 %all-gather.6.cloned.1.call-start = ((), (), s32[]{:S(2)}) async-start(), calls=%async_computation.2 | async-start | bytes 4259840 | tf_op jit(solution)/shard_map/all_gather | solution.py:24
  348.4 2.2 copy-start.3
Sparse Core Ops, SparseCore 0:
  10.3 174.8 all-gather.3
  203.7 141.2 all-gather.5
where the time goes:
time: 360 us
  waiting for transfers between devices  243 us (68%)
  blocking collectives  72.5 us (20%)
  matrix products  14.4 us (4%)
  between operations  13.6 us (4%)
  other arithmetic  8.6 us (2%)
  starting transfers between devices  4.81 us (1%)
    all_gather x2, waiting for transfers between devices, sent_together(): lax.all_gather(both, axis, axis=dim, tiled=True)  240 us
    all_gather x1, blocking collectives, body(): lax.all_gather(query_times, 'seq', axis=0, tiled=True)  72.5 us
  transfers between devices with their start and end apart: 3, of which 3 were waited for; matrix products, arithmetic and copies ran while one was open for 1% of the time, Pallas kernels for 0%

commit v1 on v0

v1 whole, which is shorter than its diff:
```python
import math

import jax
import jax.numpy as jnp
from jax import lax
from jax.experimental import pallas as pl
from jax.experimental.pallas import tpu as pltpu
from jax.sharding import PartitionSpec as P

HEADS = 16
KV_HEADS = 4
HEAD_DIM = 128
STREAMS = 3
FRAMES = 32
EPS = 1e-06
MESH = pl.DeviceIdType.MESH

Z, Y, X = 16, 4, 4
ROWS = 128
SHARD = 64
HALF = ROWS // 2
DEPTH = Z * SHARD
COLS = 3 * HEAD_DIM
META = 128
KEYS = Z * ROWS
KROWS = ROWS + 16
NEG = -1e30

ORDER = [0]
for _k in range(1, Z // 2):
    ORDER += [_k, -_k]
ORDER.append(Z // 2)
POS = {o: i for i, o in enumerate(ORDER)}
POS[-Z // 2] = POS[Z // 2]


def to_row(col):
    return jnp.transpose(jnp.broadcast_to(col, (ROWS, 128)))[0:8, :]


def to_cols(row):
    return jnp.transpose(jnp.broadcast_to(row, (128, ROWS)))


def kernel(
    x_hbm, wq_hbm, wkv_hbm, qgain, kgain, meta, keymeta, out,
    xv, xpk, xall, wall, hot, acc_kv, acc_q, in_kv, in_q, statk, statq,
    kv2, qall, ktime, obuf, oin, lbuf, lin,
    load_sem, w_ss, w_rs, x_ss, x_rs, xp_ss, xp_rs, kv_ss, kv_rs, q_ss, q_rs,
    sk_ss, sk_rs, sq_ss, sq_rs, g_ss, g_rs, p_ss, p_rs, qa_ss, qa_rs,
    o_ss, o_rs, l_ss, l_rs,
):
    h = lax.axis_index("head")
    s = lax.axis_index("seq")
    x, c = h // 2, h % 2
    z, y = s // Y, s % Y

    def zdev(d):
        return (h, lax.rem(z + d + Z, Z) * Y + y)

    def ydev(d):
        return (h, z * Y + lax.rem(y + d + Y, Y))

    def hdev(d):
        return (lax.rem(h + d, 2 * X), s)

    def xdev(d):
        return (lax.rem(h + 2 * d, 2 * X), s)

    partner = (2 * x + 1 - c, s)

    def remote(src, dst, ss, rs, dev):
        return pltpu.make_async_remote_copy(
            src_ref=src, dst_ref=dst, send_sem=ss, recv_sem=rs,
            device_id=dev, device_id_type=MESH,
        )

    x_load = pltpu.make_async_copy(x_hbm, xv, load_sem.at[0])
    wq_load = pltpu.make_async_copy(
        wq_hbm, wall.at[:, pl.ds(0, SHARD), pl.ds(HEAD_DIM, 2 * HEAD_DIM)], load_sem.at[1])
    kv_off = pl.multiple_of((2 * x + c) * HEAD_DIM, HEAD_DIM)
    wkv_load = pltpu.make_async_copy(
        wkv_hbm.at[:, :, pl.ds(kv_off, HEAD_DIM)],
        wall.at[:, pl.ds(0, SHARD), pl.ds(0, HEAD_DIM)], load_sem.at[2])
    wkv_load.start()
    wq_load.start()
    x_load.start()
    barrier = pltpu.get_barrier_semaphore()
    peers = [zdev(d) for d in (1, -1, 2, -2, 3, -3)]
    peers += [ydev(d) for d in (1, 2, 3)]
    peers += [hdev(d) for d in range(1, 2 * X)]
    for dev in peers:
        pl.semaphore_signal(barrier, inc=1, device_id=dev, device_id_type=MESH)
    wkv_load.wait()
    wq_load.wait()
    pl.semaphore_wait(barrier, len(peers))

    def w_copy(k, j, up):
        sign = -1 if up else 1
        src = wall.at[j, pl.ds(POS[sign * (k - 1)] * SHARD, SHARD)]
        dst = wall.at[j, pl.ds(POS[sign * k] * SHARD, SHARD)]
        i = 0 if up else 1
        return remote(src, dst, w_ss.at[i, k - 1, j], w_rs.at[i, k - 1, j], zdev(1 if up else -1))

    last = Z // 2
    ways = {}
    for k in range(1, last):
        ways[k] = [(j, up) for j in range(STREAMS) for up in (True, False)]
    ways[last] = [(0, True), (2, False), (1, True)]
    w_live = {}

    def w_step(k):
        for j, up in ways[k]:
            if k > 1:
                w_live[(k - 1, j, up)].wait_recv()
            w_live[(k, j, up)] = w_copy(k, j, up)
            w_live[(k, j, up)].start()
        if k == last:
            for j, up in ways[k - 1]:
                if (j, up) not in ways[k]:
                    w_live[(k - 1, j, up)].wait_recv()

    sends = []

    def sent(copy):
        copy.start()
        sends.append(copy)
        return copy

    w_step(1)

    x_load.wait()
    for t in range(Y):
        half = t % 2
        for pair in range(Z // 2):
            parts = []
            for o in (ORDER[2 * pair], ORDER[2 * pair + 1]):
                tile = 2 * lax.rem(z + o + Z, Z) + t // 2
                block = xv[:, pl.ds(pl.multiple_of(tile * 128, 128), 128)]
                parts.append(block[:, half * SHARD:(half + 1) * SHARD])
            xpk[t, :, pl.ds(pair * 128, 128)] = jnp.concatenate(parts, axis=1)
        xpk[t, :, pl.ds(DEPTH, META)] = meta[...]
    w_step(2)
    my_half = pl.ds(pl.multiple_of(c * HALF, HALF), HALF)
    x_live = {}
    for d in (2, 1, 3):
        x_live[d] = sent(remote(
            xpk.at[lax.rem(y + d, Y), my_half], xall.at[d, my_half],
            x_ss.at[d - 1], x_rs.at[d - 1], ydev(d)))
    xall[0] = xpk[y]
    w_step(3)
    w_step(4)
    xp_live = []
    for d in (1, 3, 2):
        x_live[d].wait_recv()
        xp_live.append(sent(remote(
            xall.at[d, my_half], xall.at[d, my_half],
            xp_ss.at[d - 1], xp_rs.at[d - 1], partner)))
    w_step(5)
    for copy in xp_live:
        copy.wait_recv()
    for d in range(Y):
        sid = xall[d, :, pl.ds(DEPTH, META)][:, 0:1].astype(jnp.float32)
        for j in range(STREAMS):
            on = jnp.where(sid == jnp.float32(j), jnp.float32(1.0), jnp.float32(0.0))
            hot[j, pl.ds(d * ROWS, ROWS)] = jnp.broadcast_to(on, (ROWS, 256)).astype(jnp.bfloat16)

    def project(g):
        span = pl.ds(g * 256, 256)
        for d in range(Y):
            xs = xall[d, :, span]
            total = None
            for j in range(STREAMS):
                part = jnp.dot(
                    xs * hot[j, pl.ds(d * ROWS, ROWS)], wall[j, span, :],
                    preferred_element_type=jnp.float32)
                total = part if total is None else total + part
            if g == 0:
                acc_kv[d] = total[:, :HEAD_DIM]
                acc_q[d] = total[:, HEAD_DIM:]
            else:
                acc_kv[d] += total[:, :HEAD_DIM]
                acc_q[d] += total[:, HEAD_DIM:]

    project(0)
    w_step(6)
    project(1)
    w_step(7)
    project(2)
    w_step(8)
    for j, up in ways[last]:
        w_live[(last, j, up)].wait_recv()
    project(3)

    kv_live, q_live = [], []
    for d in (2, 1, 3):
        kv_live.append(sent(remote(
            acc_kv.at[d], in_kv.at[d - 1], kv_ss.at[d - 1], kv_rs.at[d - 1], ydev(-d))))
    for d in (2, 1, 3):
        q_live.append(sent(remote(
            acc_q.at[d], in_q.at[d - 1], q_ss.at[d - 1], q_rs.at[d - 1], ydev(-d))))
    for copy in kv_live:
        copy.wait_recv()
    kv = (acc_kv[0] + in_kv[0]) + (in_kv[1] + in_kv[2])
    statk[0] = to_row(jnp.sum(kv * kv, axis=1, keepdims=True))
    sk_live = []
    for d in (2, 1, 3):
        sk_live.append(sent(remote(
            statk.at[0], statk.at[d], sk_ss.at[d - 1], sk_rs.at[d - 1], xdev(d))))
    sid = meta[:, 0:1].astype(jnp.float32)
    k_scale = jnp.zeros((ROWS, HEAD_DIM), jnp.float32)
    q_scale = jnp.zeros((ROWS, 2 * HEAD_DIM), jnp.float32)
    group = pl.ds(pl.multiple_of(x * HEAD_DIM, HEAD_DIM), HEAD_DIM)
    for j in range(STREAMS):
        k_scale = jnp.where(sid == jnp.float32(j), kgain[j:j + 1, group], k_scale)
        q_scale = jnp.where(sid == jnp.float32(j), qgain[j:j + 1, :], q_scale)
    for copy in sk_live:
        copy.wait_recv()
    k_sq = (statk[0] + statk[1]) + (statk[2] + statk[3])
    k_rs = to_cols(lax.rsqrt(k_sq / (KV_HEADS * HEAD_DIM) + EPS)[0:1, :])
    is_key = c == 0
    normed = jnp.where(is_key, kv * k_rs * k_scale, kv)
    kv2[c, 0, pl.ds(0, ROWS)] = normed.astype(jnp.bfloat16)
    kv2[c, 0, pl.ds(ROWS, 16)] = keymeta[...]

    g_live, p_live = {}, {}
    full = pl.ds(0, KROWS)

    def g_send(have, step, rows=full, index=None):
        o = have - step
        o = o - Z if o > Z // 2 else o
        i = POS[o] if index is None else index
        g_live[i] = sent(remote(
            kv2.at[c, POS[have], rows], kv2.at[c, POS[o], rows],
            g_ss.at[i], g_rs.at[i], zdev(step)))

    def p_send(have):
        i = POS[have]
        p_live[i] = sent(remote(kv2.at[c, i], kv2.at[c, i], p_ss.at[i], p_rs.at[i], partner))

    def g_wait(o):
        g_live[POS[o]].wait_recv()

    for step in (3, -3, 1, -1):
        g_send(0, step)
    p_send(0)

    for copy in q_live:
        copy.wait_recv()
    q = (acc_q[0] + in_q[0]) + (in_q[1] + in_q[2])
    statq[0] = to_row(jnp.sum(q * q, axis=1, keepdims=True))
    sq_live = []
    for d in range(1, 2 * X):
        sq_live.append(sent(remote(
            statq.at[0], statq.at[d], sq_ss.at[d - 1], sq_rs.at[d - 1], hdev(d))))
    g_wait(3)
    g_send(3, -3)
    g_send(3, 1)
    g_send(3, -1)
    g_wait(-3)
    g_send(-3, 3)
    g_send(-3, -1)
    g_send(-3, 1)
    p_send(3)
    p_send(-3)
    for o in (1, -1):
        g_wait(o)
        p_send(o)
    for copy in sq_live:
        copy.wait_recv()
    q_sq = statq[0]
    for d in range(1, 2 * X):
        q_sq = q_sq + statq[d]
    q_rs = to_cols(lax.rsqrt(q_sq / (HEADS * HEAD_DIM) + EPS)[0:1, :])
    q_rs = jnp.concatenate([q_rs, q_rs], axis=1)
    qall[0] = (q * q_rs * q_scale).astype(jnp.bfloat16)
    qa_live = []
    for d in (2, 1, 3):
        qa_live.append(sent(remote(
            qall.at[0], qall.at[d], qa_ss.at[d - 1], qa_rs.at[d - 1], ydev(d))))
    low, high = pl.ds(0, HALF), pl.ds(HALF, KROWS - HALF)
    g_wait(6)
    g_send(6, -2, low, Z - 1)
    g_send(6, 1)
    g_send(6, -1)
    g_wait(-6)
    g_send(-6, 2, high, Z)
    g_send(-6, -1)
    g_send(-6, 1)
    p_send(6)
    p_send(-6)
    for o in (2, 4, -2, -4, 5, 7, -5, -7):
        g_wait(o)
        p_send(o)
    g_live[Z - 1].wait_recv()
    g_live[Z].wait_recv()
    p_send(Z // 2)
    for copy in qa_live:
        copy.wait_recv()
    for copy in p_live.values():
        copy.wait_recv()

    for i in range(Z):
        km = kv2[0, i, pl.ds(ROWS, 16)].astype(jnp.float32)
        ktime[0:1, pl.ds(i * ROWS, ROWS)] = km[1:2, :] * FRAMES + km[0:1, :]

    score_scale = 1.0 / math.sqrt(HEAD_DIM)

    def o_copy(d):
        return remote(obuf.at[d], oin.at[d], o_ss.at[d], o_rs.at[d], ydev(-d))

    def l_copy(d):
        return remote(lbuf.at[d], lin.at[d], l_ss.at[d], l_rs.at[d], ydev(-d))

    def attend(i, carry):
        d = Y - 1 - i
        qm = xall[d, :, pl.ds(DEPTH, META)].astype(jnp.float32)
        qtime = qm[:, 64:65] * FRAMES + qm[:, 32:33]
        keys = kv2[0, :, pl.ds(0, ROWS), :].reshape(KEYS, HEAD_DIM)
        values = kv2[1, :, pl.ds(0, ROWS), :].reshape(KEYS, HEAD_DIM)
        for n in range(2):
            qn = qall[d, :, pl.ds(n * HEAD_DIM, HEAD_DIM)]
            scores = lax.dot_general(
                qn, keys, (((1,), (1,)), ((), ())), preferred_element_type=jnp.float32)
            scores = jnp.where(ktime[0:1, :] <= qtime, scores * score_scale, NEG)
            peak = jnp.max(scores, axis=1, keepdims=True)
            terms = jnp.exp(scores - peak)
            total = jnp.sum(terms, axis=1, keepdims=True)
            mixed = jnp.dot(
                terms.astype(jnp.bfloat16), values, preferred_element_type=jnp.float32)
            obuf[d, :, pl.ds(n * HEAD_DIM, HEAD_DIM)] = (mixed / total).astype(jnp.bfloat16)
            lse = jnp.where(peak > 0.5 * NEG, peak + jnp.log(total), NEG)
            lbuf[d, pl.ds(n * 8, 8)] = to_row(lse)

        @pl.when(d > 0)
        def _():
            o_copy(d).start()
            l_copy(d).start()

        return carry

    lax.fori_loop(0, Y, attend, 0)
    oin[0] = obuf[0]
    lin[0] = lbuf[0]
    for d in range(1, Y):
        o_copy(d).wait_recv()
        l_copy(d).wait_recv()
    top = jnp.maximum(jnp.maximum(lin[0], lin[1]), jnp.maximum(lin[2], lin[3]))
    weights = [jnp.exp(lin[d] - top) for d in range(Y)]
    norm = 1.0 / ((weights[0] + weights[1]) + (weights[2] + weights[3]))
    for n in range(2):
        span = pl.ds(n * HEAD_DIM, HEAD_DIM)
        result = None
        for d in range(Y):
            w = to_cols((weights[d] * norm)[n * 8:n * 8 + 1, :])
            part = w * oin[d, :, span].astype(jnp.float32)
            result = part if result is None else result + part
        out[:, span] = result.astype(jnp.bfloat16)

    for copy in w_live.values():
        copy.wait_send()
    for copy in sends:
        copy.wait_send()
    for d in range(1, Y):
        o_copy(d).wait_send()
        l_copy(d).wait_send()


def body(activations, w_query, w_keyval, q_gain, k_gain, stream_ids, local_times, block_map):
    position = lax.axis_index("seq")
    lane = lax.broadcasted_iota(jnp.int32, (ROWS, META), 1)
    row_block = 2 * position + jnp.arange(ROWS, dtype=jnp.int32) // (ROWS // 2)
    match = row_block[:, None] == jnp.arange(block_map.shape[0], dtype=jnp.int32)[None, :]
    place = jnp.sum(jnp.where(match, block_map[None, :], 0), axis=1)
    meta = jnp.where(
        lane < 32, stream_ids[:, None], jnp.where(lane < 64, local_times[:, None], place[:, None])
    ).astype(jnp.bfloat16)
    line = lax.broadcasted_iota(jnp.int32, (16, ROWS), 0)
    keymeta = jnp.where(line == 0, local_times[None, :], place[None, :]).astype(jnp.bfloat16)

    bf, f32 = jnp.bfloat16, jnp.float32
    vmem = pl.BlockSpec(memory_space=pltpu.VMEM)
    anywhere = pl.BlockSpec(memory_space=pl.ANY)
    dma = pltpu.SemaphoreType.DMA
    scratch = [
        pltpu.VMEM((ROWS, 4096), bf),
        pltpu.VMEM((Y, ROWS, DEPTH + META), bf),
        pltpu.VMEM((Y, ROWS, DEPTH + META), bf),
        pltpu.VMEM((STREAMS, DEPTH, COLS), bf),
        pltpu.VMEM((STREAMS, Y * ROWS, 256), bf),
        pltpu.VMEM((Y, ROWS, HEAD_DIM), f32),
        pltpu.VMEM((Y, ROWS, 2 * HEAD_DIM), f32),
        pltpu.VMEM((Y - 1, ROWS, HEAD_DIM), f32),
        pltpu.VMEM((Y - 1, ROWS, 2 * HEAD_DIM), f32),
        pltpu.VMEM((X, 8, ROWS), f32),
        pltpu.VMEM((2 * X, 8, ROWS), f32),
        pltpu.VMEM((2, Z, KROWS, HEAD_DIM), bf),
        pltpu.VMEM((Y, ROWS, 2 * HEAD_DIM), bf),
        pltpu.VMEM((8, KEYS), f32),
        pltpu.VMEM((Y, ROWS, 2 * HEAD_DIM), bf),
        pltpu.VMEM((Y, ROWS, 2 * HEAD_DIM), bf),
        pltpu.VMEM((Y, 16, ROWS), f32),
        pltpu.VMEM((Y, 16, ROWS), f32),
        dma((3,)),
        dma((2, Z // 2, STREAMS)), dma((2, Z // 2, STREAMS)),
    ]
    for n in (3, 3, 3, 3, 3, 7, Z + 1, Z, 3, 4, 4):
        scratch += [dma((n,)), dma((n,))]
    return pl.pallas_call(
        kernel,
        out_shape=jax.ShapeDtypeStruct((ROWS, 2 * HEAD_DIM), bf),
        in_specs=[anywhere, anywhere, anywhere, vmem, vmem, vmem, vmem],
        out_specs=vmem,
        scratch_shapes=scratch,
        compiler_params=pltpu.CompilerParams(
            collective_id=0, has_side_effects=True, vmem_limit_bytes=56 << 20),
        name="duplex_attention",
    )(activations, w_query, w_keyval, q_gain, k_gain, meta, keymeta)


def solution(mesh):
    placed = (
        P("seq", None),
        P(None, "seq", "head"),
        P(None, "seq", None),
        P(None, "head"),
        P(),
        P("seq"),
        P("seq"),
        P(),
    )
    return jax.shard_map(
        body, mesh=mesh, in_specs=placed, out_specs=P("seq", "head"), check_vma=False
    )
```

time: 360 us -> 85.6 us (0.24)
  the two profiles are of different devices: /device:TPU:4 before, /device:TPU:1 now
where the time goes in v1:
time: 85.6 us; the launch traced here: 85.4 us
  Pallas kernels  81 us (95%)
  local copies, waits for them, and re-layouts  2.78 us (3%)
  other arithmetic  1.59 us (2%)
    pallas_call x1, Pallas kernels, body(): pl.pallas_call(kernel, out_shape=jax.ShapeDtypeStruct((ROWS, 2 * HEAD_DIM...  81 us
    unnamed x7, local copies, waits for them, and re-layouts  2.78 us

profile of v1, /device:TPU:1, one launch (start us, length us, event | category | flops | bytes accessed | tf_op | source)
XLA Modules:
  0.0 85.4 jit_solution(1296957037203260748)
XLA Ops:
  0.0 0.0 copy-start.2
  0.0 0.6 copy-done.2
  0.7 0.2 select_reduce_fusion
  0.9 0.0 copy-start
  0.9 0.6 copy-done
  1.5 0.0 copy-start.1
  1.5 0.7 select_convert_fusion.1.keymeta
  2.2 0.0 copy-done.1
  2.2 0.7 select_convert_fusion.meta
  2.9 81.0 %duplex_attention.1 = bf16[128,256]{1,0:T(8,128)(2,1)} custom-call(bf16[128,4096]{1,0:T(8,128)(2,1)} %x_hbm.1, bf16[3,64,256]{2,1,0:T(8,128)(2,1)} %wq_hbm.1, bf16[3,64,1024]{2,1,0:T(8,128)(2,1)} %wkv_hbm.1, f32[3,256]{1,0:T(4,128)} %qgain.1, f32[3,512]{1,0:T(4,128)} %kgain.1, bf16[128,128]{1,0:T(8,128)(2,1)} %select_convert_fusion.meta, ...), custom_call_target="tpu_custom_call" | custom-call | tf_op jit(solution)/shard_map/duplex_attention/pallas_call | solution.py:409
  83.9 1.5 %copy.10 = bf16[128,256]{1,0:T(8,128)(2,1)} copy(bf16[128,256]{1,0:T(8,128)(2,1)} %duplex_attention.1) | data formatting | bytes 131072
  (3 shorter events, 0.0 us)
Async XLA Ops:
  0.0 0.7 copy-start.2
  0.9 0.7 copy-start
  1.5 0.7 copy-start.1

commit v2 on v1

--- a/solution.py
+++ b/solution.py
@@ -20,7 +20,6 @@
 SHARD = 64
 HALF = ROWS // 2
 DEPTH = Z * SHARD
-COLS = 3 * HEAD_DIM
 META = 128
 KEYS = Z * ROWS
 KROWS = ROWS + 16
@@ -43,8 +42,8 @@
 
 
 def kernel(
-    x_hbm, wq_hbm, wkv_hbm, qgain, kgain, meta, keymeta, out,
-    xv, xpk, xall, wall, hot, acc_kv, acc_q, in_kv, in_q, statk, statq,
+    x_hbm, wq_hbm, wkv_hbm, qg_hbm, kg_hbm, ids_hbm, times_hbm, map_hbm, out,
+    xv, qgain, kgain, ids, times, places, meta, xpk, xall, wall, wkv, hot, acc_kv, acc_q, in_kv, in_q, statk, statq,
     kv2, qall, ktime, obuf, oin, lbuf, lin,
     load_sem, w_ss, w_rs, x_ss, x_rs, xp_ss, xp_rs, kv_ss, kv_rs, q_ss, q_rs,
     sk_ss, sk_rs, sq_ss, sq_rs, g_ss, g_rs, p_ss, p_rs, qa_ss, qa_rs,
@@ -75,38 +74,98 @@
             device_id=dev, device_id_type=MESH,
         )
 
-    x_load = pltpu.make_async_copy(x_hbm, xv, load_sem.at[0])
-    wq_load = pltpu.make_async_copy(
-        wq_hbm, wall.at[:, pl.ds(0, SHARD), pl.ds(HEAD_DIM, 2 * HEAD_DIM)], load_sem.at[1])
     kv_off = pl.multiple_of((2 * x + c) * HEAD_DIM, HEAD_DIM)
-    wkv_load = pltpu.make_async_copy(
-        wkv_hbm.at[:, :, pl.ds(kv_off, HEAD_DIM)],
-        wall.at[:, pl.ds(0, SHARD), pl.ds(0, HEAD_DIM)], load_sem.at[2])
-    wkv_load.start()
-    wq_load.start()
-    x_load.start()
+    w_loads = [
+        (wkv_hbm.at[j, :, pl.ds(kv_off, HEAD_DIM)],
+         wkv.at[pl.ds(0, SHARD), pl.ds(j * HEAD_DIM, HEAD_DIM)])
+        for j in range(STREAMS)
+    ]
+    w_loads.append((wq_hbm, wall.at[:, pl.ds(0, SHARD)]))
+    row_loads = [
+        (x_hbm, xv), (ids_hbm, ids), (times_hbm, times), (map_hbm, places),
+        (qg_hbm, qgain), (kg_hbm, kgain),
+    ]
+    loads = [
+        pltpu.make_async_copy(src, dst, load_sem.at[i])
+        for i, (src, dst) in enumerate(w_loads + row_loads)
+    ]
+    for load in loads:
+        load.start()
     barrier = pltpu.get_barrier_semaphore()
-    peers = [zdev(d) for d in (1, -1, 2, -2, 3, -3)]
+    peers = [zdev(d) for d in (1, -1, 2, -2, 3, -3, 6, -6)]
     peers += [ydev(d) for d in (1, 2, 3)]
     peers += [hdev(d) for d in range(1, 2 * X)]
     for dev in peers:
         pl.semaphore_signal(barrier, inc=1, device_id=dev, device_id_type=MESH)
-    wkv_load.wait()
-    wq_load.wait()
+    for load in loads[:len(w_loads)]:
+        load.wait()
     pl.semaphore_wait(barrier, len(peers))
+
+    sends = []
+
+    def sent(copy):
+        copy.start()
+        sends.append(copy)
+        return copy
+
+    class Spread:
+        def __init__(self, piece, ss, rs):
+            self.piece, self.ss, self.rs, self.live = piece, ss, rs, {}
+
+        def send(self, have, step, part=0, index=None):
+            o = have - step
+            o = o - Z if o > Z // 2 else o
+            i = POS[o] if index is None else index
+            self.live[i] = sent(remote(
+                self.piece(POS[have], part), self.piece(POS[o], part),
+                self.ss.at[i], self.rs.at[i], zdev(step)))
+
+        def wait(self, o):
+            self.live[POS[o]].wait_recv()
+
+        def first(self):
+            for step in (6, -6, 3, -3, 1, -1):
+                self.send(0, step)
+
+        def second(self):
+            for o in (3, -3):
+                self.wait(o)
+                self.send(o, 1)
+                self.send(o, -1)
+
+        def third(self):
+            for o in (6, -6):
+                self.wait(o)
+                self.send(o, 1)
+                self.send(o, -1)
+            self.send(6, -2, 1, Z - 1)
+            self.send(-6, 2, 2, Z)
+
+        def wait_last(self):
+            self.live[Z - 1].wait_recv()
+            self.live[Z].wait_recv()
+
+    def kv_piece(i, part):
+        start, size = ((0, KROWS), (0, HALF), (HALF, KROWS - HALF))[part]
+        return kv2.at[c, i, pl.ds(start, size)]
+
+    kv_spread = Spread(kv_piece, g_ss, g_rs)
+
+    def w_piece(i, j):
+        span = pl.ds(i * SHARD, SHARD)
+        return wkv.at[span] if j == 0 else wall.at[j - 1, span]
 
     def w_copy(k, j, up):
         sign = -1 if up else 1
-        src = wall.at[j, pl.ds(POS[sign * (k - 1)] * SHARD, SHARD)]
-        dst = wall.at[j, pl.ds(POS[sign * k] * SHARD, SHARD)]
+        src, dst = w_piece(POS[sign * (k - 1)], j), w_piece(POS[sign * k], j)
         i = 0 if up else 1
         return remote(src, dst, w_ss.at[i, k - 1, j], w_rs.at[i, k - 1, j], zdev(1 if up else -1))
 
     last = Z // 2
     ways = {}
     for k in range(1, last):
-        ways[k] = [(j, up) for j in range(STREAMS) for up in (True, False)]
-    ways[last] = [(0, True), (2, False), (1, True)]
+        ways[k] = [(j, up) for j in range(STREAMS + 1) for up in (True, False)]
+    ways[last] = [(0, True), (1, False), (2, True), (3, False)]
     w_live = {}
 
     def w_step(k):
@@ -115,21 +174,31 @@
                 w_live[(k - 1, j, up)].wait_recv()
             w_live[(k, j, up)] = w_copy(k, j, up)
             w_live[(k, j, up)].start()
-        if k == last:
-            for j, up in ways[k - 1]:
-                if (j, up) not in ways[k]:
-                    w_live[(k - 1, j, up)].wait_recv()
-
-    sends = []
-
-    def sent(copy):
-        copy.start()
-        sends.append(copy)
-        return copy
+
+    def w_done(j):
+        for k in (last - 1, last):
+            for i, up in ways[k]:
+                if i == j and (k == last or (j, up) not in ways[last]):
+                    w_live[(k, j, up)].wait_recv()
 
     w_step(1)
-
-    x_load.wait()
+    for load in loads[len(w_loads):]:
+        load.wait()
+
+    lane = lax.broadcasted_iota(jnp.int32, (ROWS, META), 1)
+    row_lane = lax.broadcasted_iota(jnp.int32, (1, ROWS), 1)
+    block_places = places[...].astype(jnp.float32)
+    first, second = [
+        jnp.sum(jnp.where(row_lane == 2 * s + i, block_places, 0.0), axis=1, keepdims=True)
+        for i in range(2)
+    ]
+    place_row = jnp.where(row_lane < HALF, first, second)
+    time_row = times[...].astype(jnp.float32)
+    id_col = to_cols(ids[...].astype(jnp.float32))
+    meta[...] = jnp.where(
+        lane < 32, id_col, jnp.where(lane < 64, to_cols(time_row), to_cols(place_row))
+    ).astype(jnp.bfloat16)
+
     for t in range(Y):
         half = t % 2
         for pair in range(Z // 2):
@@ -140,7 +209,6 @@
                 parts.append(block[:, half * SHARD:(half + 1) * SHARD])
             xpk[t, :, pl.ds(pair * 128, 128)] = jnp.concatenate(parts, axis=1)
         xpk[t, :, pl.ds(DEPTH, META)] = meta[...]
-    w_step(2)
     my_half = pl.ds(pl.multiple_of(c * HALF, HALF), HALF)
     x_live = {}
     for d in (2, 1, 3):
@@ -148,15 +216,15 @@
             xpk.at[lax.rem(y + d, Y), my_half], xall.at[d, my_half],
             x_ss.at[d - 1], x_rs.at[d - 1], ydev(d)))
     xall[0] = xpk[y]
+    w_step(2)
     w_step(3)
-    w_step(4)
     xp_live = []
     for d in (1, 3, 2):
         x_live[d].wait_recv()
         xp_live.append(sent(remote(
             xall.at[d, my_half], xall.at[d, my_half],
             xp_ss.at[d - 1], xp_rs.at[d - 1], partner)))
-    w_step(5)
+    w_step(4)
     for copy in xp_live:
         copy.wait_recv()
     for d in range(Y):
@@ -164,6 +232,7 @@
         for j in range(STREAMS):
             on = jnp.where(sid == jnp.float32(j), jnp.float32(1.0), jnp.float32(0.0))
             hot[j, pl.ds(d * ROWS, ROWS)] = jnp.broadcast_to(on, (ROWS, 256)).astype(jnp.bfloat16)
+    w_step(5)
 
     def project(g):
         span = pl.ds(g * 256, 256)
@@ -176,26 +245,46 @@
                     preferred_element_type=jnp.float32)
                 total = part if total is None else total + part
             if g == 0:
-                acc_kv[d] = total[:, :HEAD_DIM]
-                acc_q[d] = total[:, HEAD_DIM:]
+                acc_q[d] = total
             else:
-                acc_kv[d] += total[:, :HEAD_DIM]
-                acc_q[d] += total[:, HEAD_DIM:]
-
+                acc_q[d] += total
+
+    def project_kv(d, span):
+        sid = xall[d, :, pl.ds(DEPTH, META)][:, 0:1].astype(jnp.float32)
+        every = jnp.dot(xall[d, :, span], wkv[span, :], preferred_element_type=jnp.float32)
+        part = every[:, :HEAD_DIM]
+        for j in range(1, STREAMS):
+            part = jnp.where(
+                sid == jnp.float32(j), every[:, j * HEAD_DIM:(j + 1) * HEAD_DIM], part)
+        return part
+
+    early, late = pl.ds(0, DEPTH - 256), pl.ds(DEPTH - 256, 256)
     project(0)
     w_step(6)
     project(1)
     w_step(7)
+    for d in range(Y):
+        acc_kv[d] = project_kv(d, early)
     project(2)
     w_step(8)
-    for j, up in ways[last]:
-        w_live[(last, j, up)].wait_recv()
+    k_scale = jnp.zeros((ROWS, HEAD_DIM), jnp.float32)
+    q_scale = jnp.zeros((ROWS, 2 * HEAD_DIM), jnp.float32)
+    sid = meta[:, 0:1].astype(jnp.float32)
+    group = pl.ds(pl.multiple_of(x * HEAD_DIM, HEAD_DIM), HEAD_DIM)
+    for j in range(STREAMS):
+        k_scale = jnp.where(sid == jnp.float32(j), kgain[j:j + 1, group], k_scale)
+        q_scale = jnp.where(sid == jnp.float32(j), qgain[j:j + 1, :], q_scale)
+
+    w_done(0)
+    kv_live, q_live = [], []
+    for d in (2, 1, 3, 0):
+        acc_kv[d] += project_kv(d, late)
+        if d:
+            kv_live.append(sent(remote(
+                acc_kv.at[d], in_kv.at[d - 1], kv_ss.at[d - 1], kv_rs.at[d - 1], ydev(-d))))
+    for j in range(STREAMS):
+        w_done(j + 1)
     project(3)
-
-    kv_live, q_live = [], []
-    for d in (2, 1, 3):
-        kv_live.append(sent(remote(
-            acc_kv.at[d], in_kv.at[d - 1], kv_ss.at[d - 1], kv_rs.at[d - 1], ydev(-d))))
     for d in (2, 1, 3):
         q_live.append(sent(remote(
             acc_q.at[d], in_q.at[d - 1], q_ss.at[d - 1], q_rs.at[d - 1], ydev(-d))))
@@ -207,13 +296,6 @@
     for d in (2, 1, 3):
         sk_live.append(sent(remote(
             statk.at[0], statk.at[d], sk_ss.at[d - 1], sk_rs.at[d - 1], xdev(d))))
-    sid = meta[:, 0:1].astype(jnp.float32)
-    k_scale = jnp.zeros((ROWS, HEAD_DIM), jnp.float32)
-    q_scale = jnp.zeros((ROWS, 2 * HEAD_DIM), jnp.float32)
-    group = pl.ds(pl.multiple_of(x * HEAD_DIM, HEAD_DIM), HEAD_DIM)
-    for j in range(STREAMS):
-        k_scale = jnp.where(sid == jnp.float32(j), kgain[j:j + 1, group], k_scale)
-        q_scale = jnp.where(sid == jnp.float32(j), qgain[j:j + 1, :], q_scale)
     for copy in sk_live:
         copy.wait_recv()
     k_sq = (statk[0] + statk[1]) + (statk[2] + statk[3])
@@ -221,30 +303,17 @@
     is_key = c == 0
     normed = jnp.where(is_key, kv * k_rs * k_scale, kv)
     kv2[c, 0, pl.ds(0, ROWS)] = normed.astype(jnp.bfloat16)
-    kv2[c, 0, pl.ds(ROWS, 16)] = keymeta[...]
-
-    g_live, p_live = {}, {}
-    full = pl.ds(0, KROWS)
-
-    def g_send(have, step, rows=full, index=None):
-        o = have - step
-        o = o - Z if o > Z // 2 else o
-        i = POS[o] if index is None else index
-        g_live[i] = sent(remote(
-            kv2.at[c, POS[have], rows], kv2.at[c, POS[o], rows],
-            g_ss.at[i], g_rs.at[i], zdev(step)))
+    line = lax.broadcasted_iota(jnp.int32, (16, ROWS), 0)
+    kv2[c, 0, pl.ds(ROWS, 16)] = jnp.where(line == 0, time_row, place_row).astype(jnp.bfloat16)
+
+    p_live = {}
 
     def p_send(have):
         i = POS[have]
         p_live[i] = sent(remote(kv2.at[c, i], kv2.at[c, i], p_ss.at[i], p_rs.at[i], partner))
 
-    def g_wait(o):
-        g_live[POS[o]].wait_recv()
-
-    for step in (3, -3, 1, -1):
-        g_send(0, step)
+    kv_spread.first()
     p_send(0)
-
     for copy in q_live:
         copy.wait_recv()
     q = (acc_q[0] + in_q[0]) + (in_q[1] + in_q[2])
@@ -253,18 +322,11 @@
     for d in range(1, 2 * X):
         sq_live.append(sent(remote(
             statq.at[0], statq.at[d], sq_ss.at[d - 1], sq_rs.at[d - 1], hdev(d))))
-    g_wait(3)
-    g_send(3, -3)
-    g_send(3, 1)
-    g_send(3, -1)
-    g_wait(-3)
-    g_send(-3, 3)
-    g_send(-3, -1)
-    g_send(-3, 1)
+    kv_spread.second()
     p_send(3)
     p_send(-3)
     for o in (1, -1):
-        g_wait(o)
+        kv_spread.wait(o)
         p_send(o)
     for copy in sq_live:
         copy.wait_recv()
@@ -274,29 +336,20 @@
     q_rs = to_cols(lax.rsqrt(q_sq / (HEADS * HEAD_DIM) + EPS)[0:1, :])
     q_rs = jnp.concatenate([q_rs, q_rs], axis=1)
     qall[0] = (q * q_rs * q_scale).astype(jnp.bfloat16)
-    qa_live = []
+
+    def qa_copy(d):
+        return remote(qall.at[0], qall.at[d], qa_ss.at[d], qa_rs.at[d], ydev(d))
+
     for d in (2, 1, 3):
-        qa_live.append(sent(remote(
-            qall.at[0], qall.at[d], qa_ss.at[d - 1], qa_rs.at[d - 1], ydev(d))))
-    low, high = pl.ds(0, HALF), pl.ds(HALF, KROWS - HALF)
-    g_wait(6)
-    g_send(6, -2, low, Z - 1)
-    g_send(6, 1)
-    g_send(6, -1)
-    g_wait(-6)
-    g_send(-6, 2, high, Z)
-    g_send(-6, -1)
-    g_send(-6, 1)
+        qa_copy(d).start()
+    kv_spread.third()
     p_send(6)
     p_send(-6)
     for o in (2, 4, -2, -4, 5, 7, -5, -7):
-        g_wait(o)
+        kv_spread.wait(o)
         p_send(o)
-    g_live[Z - 1].wait_recv()
-    g_live[Z].wait_recv()
+    kv_spread.wait_last()
     p_send(Z // 2)
-    for copy in qa_live:
-        copy.wait_recv()
     for copy in p_live.values():
         copy.wait_recv()
 
@@ -314,6 +367,11 @@
 
     def attend(i, carry):
         d = Y - 1 - i
+
+        @pl.when(d > 0)
+        def _():
+            qa_copy(d).wait_recv()
+
         qm = xall[d, :, pl.ds(DEPTH, META)].astype(jnp.float32)
         qtime = qm[:, 64:65] * FRAMES + qm[:, 32:33]
         keys = kv2[0, :, pl.ds(0, ROWS), :].reshape(KEYS, HEAD_DIM)
@@ -362,31 +420,28 @@
     for copy in sends:
         copy.wait_send()
     for d in range(1, Y):
+        qa_copy(d).wait_send()
         o_copy(d).wait_send()
         l_copy(d).wait_send()
 
 
 def body(activations, w_query, w_keyval, q_gain, k_gain, stream_ids, local_times, block_map):
-    position = lax.axis_index("seq")
-    lane = lax.broadcasted_iota(jnp.int32, (ROWS, META), 1)
-    row_block = 2 * position + jnp.arange(ROWS, dtype=jnp.int32) // (ROWS // 2)
-    match = row_block[:, None] == jnp.arange(block_map.shape[0], dtype=jnp.int32)[None, :]
-    place = jnp.sum(jnp.where(match, block_map[None, :], 0), axis=1)
-    meta = jnp.where(
-        lane < 32, stream_ids[:, None], jnp.where(lane < 64, local_times[:, None], place[:, None])
-    ).astype(jnp.bfloat16)
-    line = lax.broadcasted_iota(jnp.int32, (16, ROWS), 0)
-    keymeta = jnp.where(line == 0, local_times[None, :], place[None, :]).astype(jnp.bfloat16)
-
     bf, f32 = jnp.bfloat16, jnp.float32
     vmem = pl.BlockSpec(memory_space=pltpu.VMEM)
     anywhere = pl.BlockSpec(memory_space=pl.ANY)
     dma = pltpu.SemaphoreType.DMA
     scratch = [
         pltpu.VMEM((ROWS, 4096), bf),
+        pltpu.VMEM((STREAMS, 2 * HEAD_DIM), f32),
+        pltpu.VMEM((STREAMS, KV_HEADS * HEAD_DIM), f32),
+        pltpu.VMEM((1, ROWS), jnp.int32),
+        pltpu.VMEM((1, ROWS), jnp.int32),
+        pltpu.VMEM((1, ROWS), jnp.int32),
+        pltpu.VMEM((ROWS, META), bf),
         pltpu.VMEM((Y, ROWS, DEPTH + META), bf),
         pltpu.VMEM((Y, ROWS, DEPTH + META), bf),
-        pltpu.VMEM((STREAMS, DEPTH, COLS), bf),
+        pltpu.VMEM((STREAMS, DEPTH, 2 * HEAD_DIM), bf),
+        pltpu.VMEM((DEPTH, STREAMS * HEAD_DIM), bf),
         pltpu.VMEM((STREAMS, Y * ROWS, 256), bf),
         pltpu.VMEM((Y, ROWS, HEAD_DIM), f32),
         pltpu.VMEM((Y, ROWS, 2 * HEAD_DIM), f32),
@@ -401,21 +456,24 @@
         pltpu.VMEM((Y, ROWS, 2 * HEAD_DIM), bf),
         pltpu.VMEM((Y, 16, ROWS), f32),
         pltpu.VMEM((Y, 16, ROWS), f32),
-        dma((3,)),
-        dma((2, Z // 2, STREAMS)), dma((2, Z // 2, STREAMS)),
+        dma((10,)),
+        dma((2, Z // 2, STREAMS + 1)), dma((2, Z // 2, STREAMS + 1)),
     ]
-    for n in (3, 3, 3, 3, 3, 7, Z + 1, Z, 3, 4, 4):
+    for n in (3, 3, 3, 3, 3, 7, Z + 1, Z, 4, 4, 4):
         scratch += [dma((n,)), dma((n,))]
     return pl.pallas_call(
         kernel,
-        out_shape=jax.ShapeDtypeStruct((ROWS, 2 * HEAD_DIM), bf),
-        in_specs=[anywhere, anywhere, anywhere, vmem, vmem, vmem, vmem],
+        out_shape=pltpu.VMEM((ROWS, 2 * HEAD_DIM), bf),
+        in_specs=[anywhere] * 8,
         out_specs=vmem,
         scratch_shapes=scratch,
         compiler_params=pltpu.CompilerParams(
             collective_id=0, has_side_effects=True, vmem_limit_bytes=56 << 20),
         name="duplex_attention",
-    )(activations, w_query, w_keyval, q_gain, k_gain, meta, keymeta)
+    )(
+        activations, w_query, w_keyval, q_gain, k_gain,
+        stream_ids.reshape(1, ROWS), local_times.reshape(1, ROWS), block_map.reshape(1, ROWS),
+    )
 
 
 def solution(mesh):

time: 85.6 us -> 78.3 us (0.915)
  Pallas kernels: 81 us -> 77.5 us
  local copies, waits for them, and re-layouts: 2.78 us -> 0.63 us
  other arithmetic: 1.59 us -> 0 us
    pallas_call x1, Pallas kernels: 81 us -> 77.5 us  [body(): pl.pallas_call(kernel, out_shape=pltpu.VMEM((ROWS, 2 * HEAD_DIM), bf), in...]
    unnamed x7 -> x1, local copies, waits for them, and re-layouts: 2.78 us -> 0.63 us
    convert_element_type x2 -> x0, other arithmetic: 1.4 us -> none  [the longest x1 0.73 us: body(): meta = jnp.where(lane < 32, stream_ids[:, None], jnp.where(lane < 64, loc...]
where the time goes in v2:
time: 78.3 us; the launch traced here: 78.2 us
  Pallas kernels  77.5 us (99%)
    pallas_call x1, Pallas kernels, body(): pl.pallas_call(kernel, out_shape=pltpu.VMEM((ROWS, 2 * HEAD_DIM), bf), in...  77.5 us

profile of v2, /device:TPU:1, one launch (start us, length us, event | category | flops | bytes accessed | tf_op | source)
XLA Modules:
  0.0 78.2 jit_solution(7372967122252024744)
XLA Ops:
  0.0 77.5 %duplex_attention.1 = bf16[128,256]{1,0:T(8,128)(2,1)S(1)} custom-call(bf16[128,4096]{1,0:T(8,128)(2,1)} %x_hbm.1, bf16[3,64,256]{2,1,0:T(8,128)(2,1)} %wq_hbm.1, bf16[3,64,1024]{2,1,0:T(8,128)(2,1)} %wkv_hbm.1, f32[3,256]{1,0:T(4,128)} %qg_hbm.1, f32[3,512]{1,0:T(4,128)} %kg_hbm.1, s32[1,128]{1,0:T(1,128)} %bitcast.3, s32[1,128]{1,0:T(1,128)} %bitcast.4, ...), custom_call_target="tpu_custom_call" | custom-call | tf_op jit(solution)/shard_map/duplex_attention/pallas_call | solution.py:464
  77.6 0.6 copy.10

commit v3 on v2

--- a/solution.py
+++ b/solution.py
@@ -22,8 +22,8 @@
 DEPTH = Z * SHARD
 META = 128
 KEYS = Z * ROWS
-KROWS = ROWS + 16
 NEG = -1e30
+LOG2E = 1.0 / math.log(2.0)
 
 ORDER = [0]
 for _k in range(1, Z // 2):
@@ -44,7 +44,7 @@
 def kernel(
     x_hbm, wq_hbm, wkv_hbm, qg_hbm, kg_hbm, ids_hbm, times_hbm, map_hbm, out,
     xv, qgain, kgain, ids, times, places, meta, xpk, xall, wall, wkv, hot, acc_kv, acc_q, in_kv, in_q, statk, statq,
-    kv2, qall, ktime, obuf, oin, lbuf, lin,
+    kv2, when, qall, ktime, obuf, oin, lbuf, lin,
     load_sem, w_ss, w_rs, x_ss, x_rs, xp_ss, xp_rs, kv_ss, kv_rs, q_ss, q_rs,
     sk_ss, sk_rs, sq_ss, sq_rs, g_ss, g_rs, p_ss, p_rs, qa_ss, qa_rs,
     o_ss, o_rs, l_ss, l_rs,
@@ -92,7 +92,7 @@
     for load in loads:
         load.start()
     barrier = pltpu.get_barrier_semaphore()
-    peers = [zdev(d) for d in (1, -1, 2, -2, 3, -3, 6, -6)]
+    peers = [zdev(d) for d in (1, -1)]
     peers += [ydev(d) for d in (1, 2, 3)]
     peers += [hdev(d) for d in range(1, 2 * X)]
     for dev in peers:
@@ -146,13 +146,15 @@
             self.live[Z].wait_recv()
 
     def kv_piece(i, part):
-        start, size = ((0, KROWS), (0, HALF), (HALF, KROWS - HALF))[part]
+        start, size = ((0, ROWS), (0, HALF), (HALF, HALF))[part]
         return kv2.at[c, i, pl.ds(start, size)]
 
     kv_spread = Spread(kv_piece, g_ss, g_rs)
 
     def w_piece(i, j):
         span = pl.ds(i * SHARD, SHARD)
+        if j == STREAMS + 1:
+            return when.at[i]
         return wkv.at[span] if j == 0 else wall.at[j - 1, span]
 
     def w_copy(k, j, up):
@@ -164,12 +166,14 @@
     last = Z // 2
     ways = {}
     for k in range(1, last):
-        ways[k] = [(j, up) for j in range(STREAMS + 1) for up in (True, False)]
-    ways[last] = [(0, True), (1, False), (2, True), (3, False)]
+        ways[k] = [(j, up) for j in range(STREAMS + 2) for up in (True, False)]
+    ways[last] = [(0, True), (1, False), (2, True), (3, False), (4, True)]
     w_live = {}
 
-    def w_step(k):
+    def w_step(k, chunks=range(STREAMS + 2)):
         for j, up in ways[k]:
+            if j not in chunks:
+                continue
             if k > 1:
                 w_live[(k - 1, j, up)].wait_recv()
             w_live[(k, j, up)] = w_copy(k, j, up)
@@ -181,7 +185,7 @@
                 if i == j and (k == last or (j, up) not in ways[last]):
                     w_live[(k, j, up)].wait_recv()
 
-    w_step(1)
+    w_step(1, range(STREAMS + 1))
     for load in loads[len(w_loads):]:
         load.wait()
 
@@ -198,6 +202,10 @@
     meta[...] = jnp.where(
         lane < 32, id_col, jnp.where(lane < 64, to_cols(time_row), to_cols(place_row))
     ).astype(jnp.bfloat16)
+
+    line = lax.broadcasted_iota(jnp.int32, (16, ROWS), 0)
+    when[0] = jnp.where(line == 0, time_row, place_row).astype(jnp.bfloat16)
+    w_step(1, (STREAMS + 1,))
 
     for t in range(Y):
         half = t % 2
@@ -282,7 +290,7 @@
         if d:
             kv_live.append(sent(remote(
                 acc_kv.at[d], in_kv.at[d - 1], kv_ss.at[d - 1], kv_rs.at[d - 1], ydev(-d))))
-    for j in range(STREAMS):
+    for j in range(STREAMS + 1):
         w_done(j + 1)
     project(3)
     for d in (2, 1, 3):
@@ -302,9 +310,7 @@
     k_rs = to_cols(lax.rsqrt(k_sq / (KV_HEADS * HEAD_DIM) + EPS)[0:1, :])
     is_key = c == 0
     normed = jnp.where(is_key, kv * k_rs * k_scale, kv)
-    kv2[c, 0, pl.ds(0, ROWS)] = normed.astype(jnp.bfloat16)
-    line = lax.broadcasted_iota(jnp.int32, (16, ROWS), 0)
-    kv2[c, 0, pl.ds(ROWS, 16)] = jnp.where(line == 0, time_row, place_row).astype(jnp.bfloat16)
+    kv2[c, 0] = normed.astype(jnp.bfloat16)
 
     p_live = {}
 
@@ -322,6 +328,9 @@
     for d in range(1, 2 * X):
         sq_live.append(sent(remote(
             statq.at[0], statq.at[d], sq_ss.at[d - 1], sq_rs.at[d - 1], hdev(d))))
+    for i in range(Z):
+        km = when[i].astype(jnp.float32)
+        ktime[0:1, pl.ds(i * ROWS, ROWS)] = km[1:2, :] * FRAMES + km[0:1, :]
     kv_spread.second()
     p_send(3)
     p_send(-3)
@@ -353,10 +362,6 @@
     for copy in p_live.values():
         copy.wait_recv()
 
-    for i in range(Z):
-        km = kv2[0, i, pl.ds(ROWS, 16)].astype(jnp.float32)
-        ktime[0:1, pl.ds(i * ROWS, ROWS)] = km[1:2, :] * FRAMES + km[0:1, :]
-
     score_scale = 1.0 / math.sqrt(HEAD_DIM)
 
     def o_copy(d):
@@ -374,21 +379,24 @@
 
         qm = xall[d, :, pl.ds(DEPTH, META)].astype(jnp.float32)
         qtime = qm[:, 64:65] * FRAMES + qm[:, 32:33]
-        keys = kv2[0, :, pl.ds(0, ROWS), :].reshape(KEYS, HEAD_DIM)
-        values = kv2[1, :, pl.ds(0, ROWS), :].reshape(KEYS, HEAD_DIM)
+        keys = kv2[0].reshape(KEYS, HEAD_DIM)
+        values = kv2[1].reshape(KEYS, HEAD_DIM)
+        both = jnp.concatenate(
+            [qall[d, :, pl.ds(n * HEAD_DIM, HEAD_DIM)] for n in range(2)], axis=0)
+        scores = lax.dot_general(
+            both, keys, (((1,), (1,)), ((), ())), preferred_element_type=jnp.float32)
+        qtimes = jnp.concatenate([qtime, qtime], axis=0)
+        scores = jnp.where(ktime[0:1, :] <= qtimes, scores * (score_scale * LOG2E), NEG)
+        peak = jnp.max(scores, axis=1, keepdims=True)
+        terms = jnp.exp2(scores - peak)
+        total = jnp.sum(terms, axis=1, keepdims=True)
+        mixed = jnp.dot(terms.astype(jnp.bfloat16), values, preferred_element_type=jnp.float32)
+        mixed = (mixed / total).astype(jnp.bfloat16)
+        lse = jnp.where(peak > 0.5 * NEG, peak + jnp.log2(total), NEG)
         for n in range(2):
-            qn = qall[d, :, pl.ds(n * HEAD_DIM, HEAD_DIM)]
-            scores = lax.dot_general(
-                qn, keys, (((1,), (1,)), ((), ())), preferred_element_type=jnp.float32)
-            scores = jnp.where(ktime[0:1, :] <= qtime, scores * score_scale, NEG)
-            peak = jnp.max(scores, axis=1, keepdims=True)
-            terms = jnp.exp(scores - peak)
-            total = jnp.sum(terms, axis=1, keepdims=True)
-            mixed = jnp.dot(
-                terms.astype(jnp.bfloat16), values, preferred_element_type=jnp.float32)
-            obuf[d, :, pl.ds(n * HEAD_DIM, HEAD_DIM)] = (mixed / total).astype(jnp.bfloat16)
-            lse = jnp.where(peak > 0.5 * NEG, peak + jnp.log(total), NEG)
-            lbuf[d, pl.ds(n * 8, 8)] = to_row(lse)
+            rows = slice(n * ROWS, (n + 1) * ROWS)
+            obuf[d, :, pl.ds(n * HEAD_DIM, HEAD_DIM)] = mixed[rows]
+            lbuf[d, pl.ds(n * 8, 8)] = to_row(lse[rows])
 
         @pl.when(d > 0)
         def _():
@@ -404,7 +412,7 @@
         o_copy(d).wait_recv()
         l_copy(d).wait_recv()
     top = jnp.maximum(jnp.maximum(lin[0], lin[1]), jnp.maximum(lin[2], lin[3]))
-    weights = [jnp.exp(lin[d] - top) for d in range(Y)]
+    weights = [jnp.exp2(lin[d] - top) for d in range(Y)]
     norm = 1.0 / ((weights[0] + weights[1]) + (weights[2] + weights[3]))
     for n in range(2):
         span = pl.ds(n * HEAD_DIM, HEAD_DIM)
@@ -449,7 +457,8 @@
         pltpu.VMEM((Y - 1, ROWS, 2 * HEAD_DIM), f32),
         pltpu.VMEM((X, 8, ROWS), f32),
         pltpu.VMEM((2 * X, 8, ROWS), f32),
-        pltpu.VMEM((2, Z, KROWS, HEAD_DIM), bf),
+        pltpu.VMEM((2, Z, ROWS, HEAD_DIM), bf),
+        pltpu.VMEM((Z, 16, ROWS), bf),
         pltpu.VMEM((Y, ROWS, 2 * HEAD_DIM), bf),
         pltpu.VMEM((8, KEYS), f32),
         pltpu.VMEM((Y, ROWS, 2 * HEAD_DIM), bf),
@@ -457,7 +466,7 @@
         pltpu.VMEM((Y, 16, ROWS), f32),
         pltpu.VMEM((Y, 16, ROWS), f32),
         dma((10,)),
-        dma((2, Z // 2, STREAMS + 1)), dma((2, Z // 2, STREAMS + 1)),
+        dma((2, Z // 2, STREAMS + 2)), dma((2, Z // 2, STREAMS + 2)),
     ]
     for n in (3, 3, 3, 3, 3, 7, Z + 1, Z, 4, 4, 4):
         scratch += [dma((n,)), dma((n,))]

time: 78.3 us -> 75.1 us (0.959)
  Pallas kernels: 77.5 us -> 74.3 us
    pallas_call x1, Pallas kernels: 77.5 us -> 74.3 us  [body(): pl.pallas_call(kernel, out_shape=pltpu.VMEM((ROWS, 2 * HEAD_DIM), bf), in...]
where the time goes in v3:
time: 75.1 us; the launch traced here: 74.9 us
  Pallas kernels  74.3 us (99%)
    pallas_call x1, Pallas kernels, body(): pl.pallas_call(kernel, out_shape=pltpu.VMEM((ROWS, 2 * HEAD_DIM), bf), in...  74.3 us

profile of v3, /device:TPU:1, one launch (start us, length us, event | category | flops | bytes accessed | tf_op | source)
XLA Modules:
  0.0 74.9 jit_solution(9103480309998328536)
XLA Ops:
  0.0 74.3 %duplex_attention.1 = bf16[128,256]{1,0:T(8,128)(2,1)S(1)} custom-call(bf16[128,4096]{1,0:T(8,128)(2,1)} %x_hbm.1, bf16[3,64,256]{2,1,0:T(8,128)(2,1)} %wq_hbm.1, bf16[3,64,1024]{2,1,0:T(8,128)(2,1)} %wkv_hbm.1, f32[3,256]{1,0:T(4,128)} %qg_hbm.1, f32[3,512]{1,0:T(4,128)} %kg_hbm.1, s32[1,128]{1,0:T(1,128)} %bitcast.3, s32[1,128]{1,0:T(1,128)} %bitcast.4, ...), custom_call_target="tpu_custom_call" | custom-call | tf_op jit(solution)/shard_map/duplex_attention/pallas_call | solution.py:473
  74.3 0.6 copy.10

commit v4 on v3

--- a/solution.py
+++ b/solution.py
@@ -267,14 +267,14 @@
         return part
 
     early, late = pl.ds(0, DEPTH - 256), pl.ds(DEPTH - 256, 256)
+    w_step(6)
     project(0)
-    w_step(6)
-    project(1)
     w_step(7)
+    w_step(8)
     for d in range(Y):
         acc_kv[d] = project_kv(d, early)
+    project(1)
     project(2)
-    w_step(8)
     k_scale = jnp.zeros((ROWS, HEAD_DIM), jnp.float32)
     q_scale = jnp.zeros((ROWS, 2 * HEAD_DIM), jnp.float32)
     sid = meta[:, 0:1].astype(jnp.float32)
@@ -331,12 +331,6 @@
     for i in range(Z):
         km = when[i].astype(jnp.float32)
         ktime[0:1, pl.ds(i * ROWS, ROWS)] = km[1:2, :] * FRAMES + km[0:1, :]
-    kv_spread.second()
-    p_send(3)
-    p_send(-3)
-    for o in (1, -1):
-        kv_spread.wait(o)
-        p_send(o)
     for copy in sq_live:
         copy.wait_recv()
     q_sq = statq[0]
@@ -351,6 +345,12 @@
 
     for d in (2, 1, 3):
         qa_copy(d).start()
+    kv_spread.second()
+    p_send(3)
+    p_send(-3)
+    for o in (1, -1):
+        kv_spread.wait(o)
+        p_send(o)
     kv_spread.third()
     p_send(6)
     p_send(-6)

time: 75.1 us -> 75.1 us (level)
  no operation moved by 1% of the time
where the time goes in v4:
time: 75.1 us; the launch traced here: 74.9 us
  Pallas kernels  74.3 us (99%)
    pallas_call x1, Pallas kernels, body(): pl.pallas_call(kernel, out_shape=pltpu.VMEM((ROWS, 2 * HEAD_DIM), bf), in...  74.3 us

profile of v4, /device:TPU:1, one launch (start us, length us, event | category | flops | bytes accessed | tf_op | source)
XLA Modules:
  0.0 74.9 jit_solution(5684185080455539175)
XLA Ops:
  0.0 74.3 %duplex_attention.1 = bf16[128,256]{1,0:T(8,128)(2,1)S(1)} custom-call(bf16[128,4096]{1,0:T(8,128)(2,1)} %x_hbm.1, bf16[3,64,256]{2,1,0:T(8,128)(2,1)} %wq_hbm.1, bf16[3,64,1024]{2,1,0:T(8,128)(2,1)} %wkv_hbm.1, f32[3,256]{1,0:T(4,128)} %qg_hbm.1, f32[3,512]{1,0:T(4,128)} %kg_hbm.1, s32[1,128]{1,0:T(1,128)} %bitcast.3, s32[1,128]{1,0:T(1,128)} %bitcast.4, ...), custom_call_target="tpu_custom_call" | custom-call | tf_op jit(solution)/shard_map/duplex_attention/pallas_call | solution.py:473
  74.3 0.6 copy.10
